TPU v7x, 32 devices: a whole 2x2x4 slice. The times are simulated.
32 devices in a mesh: groups: 2 (over y), seq: 4 (over z), head: 2 (over x), rep: 2 (over core).
Axes of the slice: x: 2, y: 2, z: 4, core: 2. Of those that a mesh axis runs over, the one named last changes fastest.
Arguments:
- queries: bfloat16 [8192, 5120], P(('groups', 'seq'), ('head', 'rep')), parts along dimension 0, may hold values from -4.5 to 4.5
- keys: bfloat16 [8192, 5120], P(('groups', 'seq'), ('head', 'rep')), parts along dimension 0, may hold values from -4.5 to 4.5
- values: bfloat16 [8192, 5120], P(('groups', 'seq'), ('head', 'rep')), parts along dimension 0, may hold values from -5 to 5
- rates: float32 [40, 8192], P(('head', 'rep'), ('groups', 'seq')), parts along dimension 1, may hold values from 0.0005 to 0.005
- fast_weights: bfloat16 [128, 40, 3, 128], P(None, ('head', 'rep')), may hold values from -0.5 to 0.5
- momentum: float32 [128, 40, 3, 128], P('seq', ('head', 'rep')), may hold values from -0.3 to 0.3
Outputs:
- mixed: bfloat16 [8192, 5120], P(('groups', 'seq'), ('head', 'rep')), parts along dimension 0
- new_weights: bfloat16 [256, 40, 3, 128], P(('groups', 'seq'), ('head', 'rep')), parts along dimension 0
- new_momentum: float32 [256, 40, 3, 128], P(('groups', 'seq'), ('head', 'rep')), parts along dimension 0
There are 2 independent parts, one for each index of `groups`. A program takes and returns all parts, laid end to end along the dimension named above; an argument that names none is the same for every part. Nothing has to cross between parts.
All inputs are finite; a program needn't handle non-finite values.
Results may differ from a plain program's by a relative error of at most 0.013.
Values may be sent and summed in bfloat16 or wider, within the bound.
A program may use at most 128 MiB of HBM per device.

v0:
```python
import jax
import jax.numpy as jnp
from jax import lax
from jax.sharding import PartitionSpec as P

WIN = 512


momentum_keep = 0.9
epsilon = 1e-06


def passed_along(value, axis, by):
    peers = lax.axis_size(axis)
    pairs = [(i, i + by) for i in range(peers) if 0 <= i + by < peers]
    return lax.ppermute(value, axis, pairs)


def window_block(query_block, key_block, value_block, first):
    width = query_block.shape[0]
    head_size = query_block.shape[2]
    scores = jnp.einsum(
        "qhd,khd->hqk", query_block, key_block, preferred_element_type=jnp.float32
    ) * head_size ** (-0.5)
    query_index = jnp.arange(width, dtype=jnp.int32)[:, None]
    key_index = jnp.arange(2 * width, dtype=jnp.int32)[None, :]
    allowed = (
        (key_index > query_index) & (key_index <= query_index + width) & (key_index + first >= 0)
    )
    scores = jnp.where(allowed[None], scores, -1e30)
    row_max = jnp.max(scores, axis=-1, keepdims=True)
    weights = jnp.exp(scores - row_max)
    total = jnp.sum(weights, axis=-1, keepdims=True)
    probabilities = (weights / total).astype(jnp.bfloat16)
    return jnp.einsum(
        "hqk,khd->qhd", probabilities, value_block, preferred_element_type=jnp.float32
    )


def swiglu_parts(inputs, weights):
    inner = jnp.einsum(
        "thr,rhcf->thcf", inputs, weights[:, :, 0:2], preferred_element_type=jnp.float32
    )
    return (inner[:, :, 0], inner[:, :, 1])


def refresh(old_weights, old_momentum, grads):
    new_momentum = momentum_keep * old_momentum + grads
    before = old_weights.astype(jnp.float32)
    moved = before + new_momentum
    ratio = jnp.sqrt(
        (jnp.mean(before * before, axis=-1, keepdims=True) + epsilon)
        / (jnp.mean(moved * moved, axis=-1, keepdims=True) + epsilon)
    )
    return ((moved * ratio).astype(jnp.bfloat16), new_momentum)


def shards(queries, keys, values, rates, fast_weights, momentum):
    tok_rows = queries.shape[0]
    heads_here = rates.shape[0]
    head_size = fast_weights.shape[0]
    own_rows = momentum.shape[0]
    query_heads = queries.reshape(tok_rows, heads_here, head_size)
    key_heads = keys.reshape(tok_rows, heads_here, head_size)
    value_heads = values.reshape(tok_rows, heads_here, head_size)
    tail = jnp.stack([keys[tok_rows - WIN :], values[tok_rows - WIN :]])
    previous = passed_along(tail, "seq", 1)
    gating, upward = swiglu_parts(key_heads, fast_weights)
    sigmoid_gate = jax.nn.sigmoid(gating)
    hidden = (gating * sigmoid_gate * upward).astype(jnp.bfloat16)
    scaled_values = (value_heads.astype(jnp.float32) * jnp.transpose(rates)[:, :, None]).astype(
        jnp.bfloat16
    )
    hidden_grad = jnp.einsum(
        "thr,rhf->thf", scaled_values, fast_weights[:, :, 2], preferred_element_type=jnp.float32
    )
    gate_grad = (
        hidden_grad * upward * sigmoid_gate * (1.0 + gating * (1.0 - sigmoid_gate))
    ).astype(jnp.bfloat16)
    upward_grad = (hidden_grad * gating * sigmoid_gate).astype(jnp.bfloat16)
    paired = jnp.stack([gate_grad, upward_grad], axis=2)
    row_offset = lax.axis_index("seq") * own_rows
    first_grads = jnp.einsum(
        "thr,thcf->rhcf", key_heads, paired, preferred_element_type=jnp.float32
    )
    second_grads = jnp.einsum(
        "thr,thf->rhf", scaled_values, hidden, preferred_element_type=jnp.float32
    )[:, :, None]
    grads = lax.psum(jnp.concatenate([first_grads, second_grads], axis=2), "seq")
    whole_momentum = lax.all_gather(
        momentum.astype(jnp.bfloat16), "seq", axis=0, tiled=True
    ).astype(momentum.dtype)
    new_weights, full_momentum = refresh(fast_weights, whole_momentum, grads)
    new_rows = lax.dynamic_slice_in_dim(new_weights, row_offset, own_rows, 0)
    new_momentum = lax.dynamic_slice_in_dim(full_momentum, row_offset, own_rows, 0)
    query_gating, query_upward = swiglu_parts(query_heads, new_weights)
    query_hidden = (jax.nn.silu(query_gating) * query_upward).astype(jnp.bfloat16)
    fast_out = jnp.einsum(
        "thf,rhf->thr", query_hidden, new_weights[:, :, 2], preferred_element_type=jnp.float32
    )
    extended_keys = jnp.concatenate([previous[0], keys], axis=0).reshape(
        WIN + tok_rows, heads_here, head_size
    )
    extended_values = jnp.concatenate([previous[1], values], axis=0).reshape(
        WIN + tok_rows, heads_here, head_size
    )
    first_key = lax.axis_index("seq") * tok_rows - WIN

    def one_block(block):
        query_block = lax.dynamic_slice_in_dim(query_heads, block * WIN, WIN, 0)
        key_block = lax.dynamic_slice_in_dim(extended_keys, block * WIN, 2 * WIN, 0)
        value_block = lax.dynamic_slice_in_dim(extended_values, block * WIN, 2 * WIN, 0)
        return window_block(query_block, key_block, value_block, first_key + block * WIN)

    attended = lax.map(one_block, jnp.arange(tok_rows // WIN, dtype=jnp.int32)).reshape(
        tok_rows, heads_here, head_size
    )
    mixed = (fast_out + attended).reshape(tok_rows, heads_here * head_size).astype(jnp.bfloat16)
    return (mixed, new_rows, new_momentum)


def solution(mesh):
    return jax.shard_map(
        shards,
        mesh=mesh,
        in_specs=(
            P(("groups", "seq"), ("head", "rep")),
            P(("groups", "seq"), ("head", "rep")),
            P(("groups", "seq"), ("head", "rep")),
            P(("head", "rep"), ("groups", "seq")),
            P(None, ("head", "rep"), None, None),
            P("seq", ("head", "rep"), None, None),
        ),
        out_specs=(
            P(("groups", "seq"), ("head", "rep")),
            P(("groups", "seq"), ("head", "rep"), None, None),
            P(("groups", "seq"), ("head", "rep"), None, None),
        ),
        check_vma=False,
    )
```

profile of v0, /device:TPU:0, one launch (start us, length us, event | category | flops | bytes accessed | tf_op | source)
XLA Modules:
  0.0 385.5 jit_solution(15369249530486513735)
XLA Ops:
  7.2 4.4 %copy.53 = bf16[1024,1280]{0,1:T(8,128)(2,1)} copy(bf16[1024,1280]{1,0:T(8,128)(2,1)} %param.10) | data formatting | bytes 5242880 | tf_op args[2]
  11.6 3.0 copy.57
  16.8 2.8 convolution_bitcast_fusion.1
  19.7 2.3 fusion.54
  22.0 4.3 %fusion.46 = (bf16[1024,10,1,128]{3,0,1,2:T(8,128)(2,1)S(1)}, bf16[1024,10,1,128]{3,0,1,2:T(8,128)(2,1)S(1)}) fusion(f32[1024,10,2,128]{3,0,1,2:T(8,128)S(1)} %convolution_bitcast_fusion.1, bf16[128,10,3,128]{3,0,2,1:T(8,128)(2,1)} %param.12, bf16[1024,10,128]{0,2,1:T(8,128)(2,1)S(1)} %bitcast.123, f32[1024,10]{0,1:T(8,128)S(1)} %bitcast.131), kind=kOutput, calls=%fused_computation.57 | convolution fusion | flops 356515840 | bytes 18718720 | tf_op jit(solution)/shard_map/thr,rhf->thf/dot_general | solution.py:74
  33.2 6.4 %collective-permute-start = (bf16[2,512,1280]{1,2,0:T(8,128)(2,1)}, bf16[2,512,1280]{1,2,0:T(8,128)(2,1)}, u32[]{:S(2)}, u32[]{:S(2)}) collective-permute-start(bf16[2,512,1280]{1,2,0:T(8,128)(2,1)} %pad_maximum_fusion.3), channel_id=1, source_target_pairs={{0,4},{4,8},{8,12},{1,5},{5,9},{9,13},{2,6},{6,10},{10,14},{3,7},{... | collective-permute-start | bytes 7864328 | tf_op jit(solution)/shard_map/ppermute | solution.py:16
  39.7 4.5 %copy.64 = bf16[1024,1280]{0,1:T(8,128)(2,1)} copy(bf16[1024,1280]{1,0:T(8,128)(2,1)} %param.8) | data formatting | bytes 5242880 | tf_op args[0]
  44.2 134.8 %all_gather.3 = bf16[128,10,3,128]{3,0,2,1:T(8,128)(2,1)} all-gather(bf16[32,10,3,128]{3,0,2,1:T(8,128)(2,1)S(1)} %convert_element_type.40), channel_id=1, replica_groups=mesh['groups'=2,'seq'=4,'head'=2,'rep'=2] {'seq'}, dimensions={0}, use_global_device_ids=true | all-gather | bytes 1228800 | tf_op jit(solution)/shard_map/all_gather | solution.py:90
  181.3 2.9 fusion.48
  190.4 3.4 constant_dynamic-slice_fusion
  193.8 2.9 copy.75
  196.7 7.5 %convolution_bitcast_fusion = f32[1024,10,2,128]{3,0,1,2:T(8,128)} fusion(bf16[1024,10,128,1]{0,2,1,3:T(8,128)(2,1)} %bitcast.125, bf16[128,10,3,128]{0,3,2,1:T(8,128)(2,1)} %copy-done.4), kind=kOutput, calls=%fused_computation.51 | convolution fusion | flops 671088640 | bytes 13762560 | tf_op jit(solution)/shard_map/thr,rhcf->thcf/dot_general | solution.py:41
  211.2 149.1 %while.10 = (s32[]{:T(128)}, f32[2,512,10,128]{1,0,3,2:T(2,128)}, s32[2]{0:T(128)S(1)}, bf16[1536,10,128]{0,2,1:T(8,128)(2,1)}, s32[]{:T(128)}, /*index=5*/bf16[...) while((s32[]{:T(128)}, f32[2,512,10,128]{1,0,3,2:T(2,128)}, ...), condition=%wide.region_6.7_spmd, body=%wide.region_3.6_spmd.sunk | while | flops 2717912576 | bytes 62699760 | solution.py:115
  212.9 13.1 %fusion.89 = (f32[10,512]{1,0:T(8,128)S(1)}, f32[10,512,1024]{2,1,0:T(8,128)}) fusion(pred[512,1024]{1,0:T(8,128)(4,1)S(1)} %fusion.88, bf16[1536,10,128]{0,2,1:T(8,128)(2,1)} %get-tuple-element.166, s32[]{:T(128)S(6)} %select_n.30, bf16[1024,10,128]{0,2,1:T(8,128)(2,1)} %get-tuple-element.165, s32[]{:T(128)S(6)} %select_n.31), kind=kOutput, calls=%fused_computation.81.clone.1 | convolution fusion | flops 1363149824 | bytes 25448456 | tf_op jit(solution)/shard_map/while/body/eval_jaxpr/sub | solution.py:32
  226.0 9.7 %fusion.90 = f32[1,512,10,128]{1,3,2,0:T(8,128)S(1)} fusion(f32[10,512,1024]{2,1,0:T(8,128)} %get-tuple-element.134, f32[10,512]{1,0:T(8,128)S(1)} %get-tuple-element.135, bf16[1536,10,128]{0,2,1:T(8,128)(2,1)} %get-tuple-element.163, s32[]{:T(128)S(6)} %select_n.30), kind=kOutput, calls=%fused_computation.18.clone.1 | convolution fusion | flops 1352663040 | bytes 26234884 | tf_op jit(solution)/shard_map/while/body/eval_jaxpr/hqk,khd->qhd/dot_general | solution.py:35
  235.8 2.7 copy.109
  238.5 47.2 %dynamic_update_slice.5 = f32[2,512,10,128]{1,0,3,2:T(2,128)} dynamic-update-slice(f32[2,512,10,128]{1,0,3,2:T(2,128)} %get-tuple-element.149, f32[1,512,10,128]{1,0,3,2:T(1,128)S(1)} %copy.109, s32[]{:T(128)S(6)} %copy.113, s32[]{:T(128)} %constant.18.clone.1..sunk, s32[]{:T(128)} %constant.18.clone.1..sunk, s32[]{:T(128)} %constant.18.clone.1..sunk) | dynamic-update-slice | bytes 5242884 | tf_op jit(solution)/shard_map/while/body/jit(dynamic_update_index_in_dim)/dynamic_update_slice | solution.py:115
  287.4 13.1 %fusion.89 = (f32[10,512]{1,0:T(8,128)S(1)}, f32[10,512,1024]{2,1,0:T(8,128)}) fusion(pred[512,1024]{1,0:T(8,128)(4,1)S(1)} %fusion.88, bf16[1536,10,128]{0,2,1:T(8,128)(2,1)} %get-tuple-element.166, s32[]{:T(128)S(6)} %select_n.30, bf16[1024,10,128]{0,2,1:T(8,128)(2,1)} %get-tuple-element.165, s32[]{:T(128)S(6)} %select_n.31), kind=kOutput, calls=%fused_computation.81.clone.1 | convolution fusion | flops 1363149824 | bytes 25448456 | tf_op jit(solution)/shard_map/while/body/eval_jaxpr/sub | solution.py:32
  300.5 9.7 %fusion.90 = f32[1,512,10,128]{1,3,2,0:T(8,128)S(1)} fusion(f32[10,512,1024]{2,1,0:T(8,128)} %get-tuple-element.134, f32[10,512]{1,0:T(8,128)S(1)} %get-tuple-element.135, bf16[1536,10,128]{0,2,1:T(8,128)(2,1)} %get-tuple-element.163, s32[]{:T(128)S(6)} %select_n.30), kind=kOutput, calls=%fused_computation.18.clone.1 | convolution fusion | flops 1352663040 | bytes 26234884 | tf_op jit(solution)/shard_map/while/body/eval_jaxpr/hqk,khd->qhd/dot_general | solution.py:35
  310.3 2.7 copy.109
  313.0 47.2 %dynamic_update_slice.5 = f32[2,512,10,128]{1,0,3,2:T(2,128)} dynamic-update-slice(f32[2,512,10,128]{1,0,3,2:T(2,128)} %get-tuple-element.149, f32[1,512,10,128]{1,0,3,2:T(1,128)S(1)} %copy.109, s32[]{:T(128)S(6)} %copy.113, s32[]{:T(128)} %constant.18.clone.1..sunk, s32[]{:T(128)} %constant.18.clone.1..sunk, s32[]{:T(128)} %constant.18.clone.1..sunk) | dynamic-update-slice | bytes 5242884 | tf_op jit(solution)/shard_map/while/body/jit(dynamic_update_index_in_dim)/dynamic_update_slice | solution.py:115
  360.2 8.1 %reshape.111 = f32[1024,10,128]{0,2,1:T(8,128)} reshape(f32[2,512,10,128]{1,0,3,2:T(2,128)} %get-tuple-element.40) | data formatting | bytes 10485760 | tf_op jit(solution)/shard_map/reshape | solution.py:115
  368.4 7.6 %fusion.34 = bf16[1024,10,128]{0,2,1:T(8,128)(2,1)S(1)} fusion(f32[1024,10,128]{0,2,1:T(8,128)} %reshape.111, f32[1024,10,2,128]{3,0,1,2:T(8,128)} %convolution_bitcast_fusion, bf16[128,10,3,128]{0,3,2,1:T(8,128)(2,1)} %copy-done.4), kind=kOutput, calls=%fused_computation.36 | convolution fusion | flops 346030080 | bytes 18677760 | tf_op jit(solution)/shard_map/thf,rhf->thr/dot_general | solution.py:98
  376.0 2.7 copy.73
  (42 shorter events, 26.6 us)
Async XLA Ops:
  7.2 174.2 %all-reduce.2.cloned.1.call-start = ((), (), s32[]{:S(2)}) async-start(), calls=%async_computation | async-start | bytes 3932160 | tf_op jit(solution)/shard_map/psum | solution.py:89
  16.8 2.8 copy-start.1
  16.8 2.8 copy-start.6
  33.2 170.9 %collective-permute-start = (bf16[2,512,1280]{1,2,0:T(8,128)(2,1)}, bf16[2,512,1280]{1,2,0:T(8,128)(2,1)}, u32[]{:S(2)}, u32[]{:S(2)}) collective-permute-start(bf16[2,512,1280]{1,2,0:T(8,128)(2,1)} %pad_maximum_fusion.3), channel_id=1, source_target_pairs={{0,4},{4,8},{8,12},{1,5},{5,9},{9,13},{2,6},{6,10},{10,14},{3,7},{... | collective-permute-start | bytes 7864328 | tf_op jit(solution)/shard_map/ppermute | solution.py:16
  39.7 4.5 %copy-start.5 = (f32[32,10,3,128]{3,0,2,1:T(8,128)S(1)}, f32[32,10,3,128]{3,0,2,1:T(8,128)}, u32[]{:S(2)}) copy-start(f32[32,10,3,128]{3,0,2,1:T(8,128)} %param.13) | copy-start | bytes 1474564
  181.3 4.2 %copy-start.3 = (bf16[128,10,3,128]{0,3,2,1:T(8,128)(2,1)S(1)}, bf16[128,10,3,128]{0,3,2,1:T(8,128)(2,1)}, u32[]{:S(2)}) copy-start(bf16[128,10,3,128]{0,3,2,1:T(8,128)(2,1)} %copy.51) | copy-start | bytes 2949124
  184.2 1.3 copy-start
  185.9 1.0 copy-start.4
  204.2 2.5 copy-start.2
Sparse Core Ops, SparseCore 0:
  30.1 138.0 all-reduce.1
where the time goes:
time: 393 us; the launch traced here: 386 us
  local copies, waits for them, and re-layouts  144 us (37%)
  blocking collectives  135 us (34%)
  matrix products  72.4 us (18%)
  between operations  14.2 us (4%)
  other arithmetic  11.8 us (3%)
  starting transfers between devices  6.47 us (2%)
    all_gather x1, blocking collectives, shards(): lax.all_gather(momentum.astype(jnp.bfloat16), 'seq', axis=0, tiled=True)  135 us
    dynamic_update_slice x4, local copies, waits for them, and re-layouts, shards(): lax.map(one_block, jnp.arange(tok_rows // WIN, dtype=jnp.int32))  99.9 us
    sub x2, matrix products, window_block(): weights = jnp.exp(scores - row_max)  26.3 us
    unnamed x21, local copies, waits for them, and re-layouts  24.7 us
    dot_general x2, matrix products, window_block(): jnp.einsum('hqk,khd->qhd', probabilities, value_block, preferred_element_...  19.5 us
    dot_general x2, matrix products, swiglu_parts(): jnp.einsum('thr,rhcf->thcf', inputs, weights[:, :, 0:2], preferred_elemen...  10.3 us
    reshape x1, local copies, waits for them, and re-layouts, shards(): lax.map(one_block, jnp.arange(tok_rows // WIN, dtype=jnp.int32))  8.14 us
  transfers between devices with their start and end apart: 2, of which 0 were waited for; matrix products, arithmetic and copies ran while one was open for 8% of the time, Pallas kernels for 0%

commit v1 on v0

v1 whole, which is shorter than its diff:
```python
import functools
import math

import jax
import jax.numpy as jnp
from jax import lax
from jax.experimental import pallas as pl
from jax.experimental.pallas import tpu as pltpu
from jax.sharding import PartitionSpec as P

WIN = 512
momentum_keep = 0.9
epsilon = 1e-06
MESH = pl.DeviceIdType.MESH
F32 = jnp.float32
BF16 = jnp.bfloat16
NEG = -1e30
ROWS = WIN // 2


def dot_nn(a, b):
    return lax.dot_general(a, b, (((1,), (0,)), ((), ())), preferred_element_type=F32)


def dot_nt(a, b):
    return lax.dot_general(a, b, (((1,), (1,)), ((), ())), preferred_element_type=F32)


def dot_tn(a, b):
    return lax.dot_general(a, b, (((0,), (0,)), ((), ())), preferred_element_type=F32)


def kernel(
    n, heads, tok, d, own,
    q_hbm, k_hbm, v_hbm, r_ref, w_ref, wown_ref, mom_ref,
    out_hbm, nw_ref, nm_ref,
    qb, kb, vb, qr, att, lse, osend, orecv, stat, ssend, srecv, outb,
    gradb, gbuf, rsbuf, wnew,
    load_sem, out_sem, qs_sem, qr_sem, os_sem, or_sem, ss_sem, sr_sem,
    rs_s, rs_r, ag_s, ag_r,
):
    me = lax.axis_index("seq")
    first = me == 0
    last = me == n - 1
    scale = math.log2(math.e) / math.sqrt(d)
    before = lax.max(me - 1, 0)
    after = lax.min(me + 1, n - 1)

    def cols(h):
        return pl.ds(pl.multiple_of(h * d, d), d)

    def load(which, h):
        src = (q_hbm, k_hbm, v_hbm)[which]
        dst = (qb, kb, vb)[which]
        return pltpu.make_async_copy(src.at[:, cols(h)], dst.at[h], load_sem.at[which, h])

    def send_query(h):
        return pltpu.make_async_remote_copy(
            src_ref=q_hbm.at[pl.ds(0, WIN), cols(h)], dst_ref=qr.at[h],
            send_sem=qs_sem.at[h], recv_sem=qr_sem.at[h],
            device_id={"seq": before}, device_id_type=MESH)

    def send_result(h):
        return pltpu.make_async_remote_copy(
            src_ref=osend.at[h], dst_ref=orecv.at[h],
            send_sem=os_sem.at[h], recv_sem=or_sem.at[h],
            device_id={"seq": after}, device_id_type=MESH)

    def send_stats():
        return pltpu.make_async_remote_copy(
            src_ref=ssend, dst_ref=srecv, send_sem=ss_sem, recv_sem=sr_sem,
            device_id={"seq": after}, device_id_type=MESH)

    def send_grad(peer, h):
        return pltpu.make_async_remote_copy(
            src_ref=gbuf.at[peer, h], dst_ref=rsbuf.at[me, h],
            send_sem=rs_s.at[peer], recv_sem=rs_r.at[me],
            device_id={"seq": peer}, device_id_type=MESH)

    def whole_grad(peer):
        return pltpu.make_async_remote_copy(
            src_ref=gbuf.at[peer], dst_ref=rsbuf.at[peer],
            send_sem=rs_s.at[peer], recv_sem=rs_r.at[peer],
            device_id={"seq": peer}, device_id_type=MESH)

    def send_weights(peer, slot):
        return pltpu.make_async_remote_copy(
            src_ref=wnew.at[me], dst_ref=wnew.at[slot],
            send_sem=ag_s.at[peer], recv_sem=ag_r.at[slot],
            device_id={"seq": peer}, device_id_type=MESH)

    def each_peer(act):
        for step in range(1, n):
            act(lax.rem(me + step, n))

    def each_head(lo, hi, act):
        def body(h, carry):
            act(h)
            return carry
        lax.fori_loop(lo, hi, body, 0)

    def start_loads(h):
        load(1, h).start()
        load(2, h).start()

    each_head(0, heads, start_loads)
    barrier = pltpu.get_barrier_semaphore()
    each_peer(lambda peer: pl.semaphore_signal(
        barrier, inc=1, device_id={"seq": peer}, device_id_type=MESH))
    pl.semaphore_wait(barrier, n - 1)
    early = heads // 2

    @pl.when(jnp.logical_not(first))
    def _():
        each_head(0, early, lambda h: send_query(h).start())

    each_head(0, heads, lambda h: load(0, h).start())
    rows = lax.broadcasted_iota(jnp.int32, (ROWS, ROWS), 0)
    columns = lax.broadcasted_iota(jnp.int32, (ROWS, ROWS), 1)
    causal = columns <= rows
    ones = jnp.ones((ROWS, d), BF16)

    def gradient(h):
        load(1, h).wait()
        load(2, h).wait()
        weights = w_ref[h]
        lane = lax.broadcasted_iota(jnp.int32, (ROWS, heads), 1)
        total = jnp.zeros((d, 3 * d), F32)
        for b in range(tok // ROWS):
            part = slice(b * ROWS, (b + 1) * ROWS)
            keys = kb[h, part]
            rate = jnp.sum(jnp.where(lane == h, r_ref[part], 0.0), axis=1, keepdims=True)
            scaled = (vb[h, part].astype(F32) * rate).astype(BF16)
            inner = dot_nn(keys, weights[:, : 2 * d])
            gating, upward = inner[:, :d], inner[:, d:]
            sig = jax.nn.sigmoid(gating)
            silu = gating * sig
            hidden_grad = dot_nn(scaled, weights[:, 2 * d :])
            gradb[part, :d] = (hidden_grad * upward * sig * (1.0 + gating * (1.0 - sig))).astype(BF16)
            gradb[part, d : 2 * d] = (hidden_grad * silu).astype(BF16)
            gradb[part, 2 * d : 3 * d] = (silu * upward).astype(BF16)
            gradb[part, 3 * d :] = scaled
        one = dot_tn(kb[h], gradb[:, : 2 * d])
        two = dot_tn(gradb[:, 3 * d :], gradb[:, 2 * d : 3 * d])
        for p in range(n):
            part = slice(p * own, (p + 1) * own)
            gbuf[p, h, :, : 2 * d] = one[part].astype(BF16)
            gbuf[p, h, :, 2 * d :] = two[part].astype(BF16)
        each_peer(lambda peer: send_grad(peer, h).start())

    each_head(0, heads, gradient)

    @pl.when(jnp.logical_not(first))
    def _():
        each_head(early, heads, lambda h: send_query(h).start())

    def with_ones(values, blocks):
        return jnp.concatenate([values, jnp.concatenate([ones] * blocks, axis=0)], axis=1)

    def finish(acc, top):
        total = jnp.maximum(acc[:, d:], 1e-30)
        return acc[:, :d] / total, top * scale + jnp.log2(total)

    def edge(query, keys, values, keep, spare):
        blocks = keys.shape[0] // ROWS
        scores = dot_nt(query, keys)
        at = spare * ROWS
        masked = jnp.where(keep, scores[:, at : at + ROWS], NEG)
        top = masked
        if blocks == 2:
            full = scores[:, (1 - spare) * ROWS : (2 - spare) * ROWS]
            top = jnp.maximum(top, full)
        top = jnp.max(top, axis=1, keepdims=True)
        p = jnp.where(keep, jnp.exp2((masked - top) * scale), 0.0).astype(BF16)
        if blocks == 2:
            f = jnp.exp2((full - top) * scale).astype(BF16)
            p = jnp.concatenate([p, f] if spare == 0 else [f, p], axis=1)
        return finish(dot_nn(p, with_ones(values, blocks)), top)

    def inside(h, b):
        span = slice((b - 2) * ROWS, (b + 1) * ROWS)
        scores = dot_nt(qb[h, b * ROWS : (b + 1) * ROWS], kb[h, span])
        mixed = jnp.where(causal, scores[:, 2 * ROWS :], scores[:, :ROWS])
        full = scores[:, ROWS : 2 * ROWS]
        top = jnp.max(jnp.maximum(mixed, full), axis=1, keepdims=True)
        pm = jnp.exp2((mixed - top) * scale)
        pf = jnp.exp2((full - top) * scale).astype(BF16)
        p = jnp.concatenate(
            [jnp.where(causal, 0.0, pm).astype(BF16), pf, jnp.where(causal, pm, 0.0).astype(BF16)],
            axis=1)
        acc = dot_nn(p, with_ones(vb[h, span], 3))
        return acc[:, :d] / acc[:, d:]

    def local(h):
        load(0, h).wait()
        for b in range(tok // ROWS):
            part = slice(b * ROWS, (b + 1) * ROWS)
            if b < 2:
                span = slice(0, (b + 1) * ROWS)
                o, s = edge(qb[h, part], kb[h, span], vb[h, span], causal, b)
                lse[h, part] = s
            else:
                o = inside(h, b)
            att[h, part] = o

    each_head(0, heads, local)
    tail = tok - WIN

    def remote(h):
        send_query(h).wait_recv()
        lane = lax.broadcasted_iota(jnp.int32, (ROWS, 128), 1)
        for b in range(2):
            part = slice(b * ROWS, (b + 1) * ROWS)
            span = slice(tail + b * ROWS, tok)
            o, s = edge(qr[h, part], kb[h, span], vb[h, span], jnp.logical_not(causal), 0)
            osend[h, part] = o.astype(BF16)
            stat[part] = jnp.where(lane == h, s, stat[part])
        send_result(h).start()

    @pl.when(jnp.logical_not(last))
    def _():
        stat[...] = jnp.zeros_like(stat)
        each_head(0, early, remote)

    each_peer(lambda peer: whole_grad(peer).wait_recv())

    def refresh(h):
        total = gbuf[me, h].astype(F32)
        for step in range(1, n):
            total = total + rsbuf[lax.rem(me + step, n), h].astype(F32)
        moment = momentum_keep * mom_ref[h] + total
        nm_ref[h] = moment
        old = wown_ref[h].astype(F32)
        moved = old + moment
        for c in range(3):
            part = slice(c * d, (c + 1) * d)
            o, m = old[:, part], moved[:, part]
            ratio = jnp.sqrt(
                (jnp.mean(o * o, axis=1, keepdims=True) + epsilon)
                / (jnp.mean(m * m, axis=1, keepdims=True) + epsilon))
            new = (m * ratio).astype(BF16)
            wnew[me, h, :, part] = new
            nw_ref[h, :, part] = new

    each_head(0, heads, refresh)
    each_peer(lambda peer: send_weights(peer, me).start())

    @pl.when(jnp.logical_not(last))
    def _():
        each_head(early, heads, remote)
        ssend[...] = jnp.transpose(stat[...])[: ssend.shape[0]]
        send_stats().start()

    each_peer(lambda peer: send_weights(peer, peer).wait_recv())

    @pl.when(jnp.logical_not(first))
    def _():
        send_stats().wait_recv()
        held = srecv[...]
        stat2 = jnp.concatenate(
            [held, jnp.zeros((128 - held.shape[0], WIN), F32)], axis=0)
        stat[...] = jnp.transpose(stat2)

    def output(h):
        @pl.when(jnp.logical_not(first))
        def _():
            send_result(h).wait_recv()
            lane = lax.broadcasted_iota(jnp.int32, (ROWS, 128), 1)
            for b in range(2):
                part = slice(b * ROWS, (b + 1) * ROWS)
                theirs = jnp.sum(jnp.where(lane == h, stat[part], 0.0), axis=1, keepdims=True)
                ours = lse[h, part]
                top = jnp.maximum(ours, theirs)
                mine = jnp.exp2(ours - top)
                other = jnp.exp2(theirs - top)
                att[h, part] = (
                    att[h, part] * mine + orecv[h, part].astype(F32) * other) / (mine + other)

        weights = jnp.concatenate(
            [wnew[p, h].astype(F32) for p in range(n)], axis=0).astype(BF16)
        for b in range(tok // ROWS):
            part = slice(b * ROWS, (b + 1) * ROWS)
            inner = dot_nn(qb[h, part], weights[:, : 2 * d])
            gating, upward = inner[:, :d], inner[:, d:]
            hidden = (gating * jax.nn.sigmoid(gating) * upward).astype(BF16)
            fast = dot_nt(hidden, weights[:, 2 * d :])
            outb[h, part] = (fast + att[h, part]).astype(BF16)
        pltpu.make_async_copy(outb.at[h], out_hbm.at[:, cols(h)], out_sem.at[h]).start()

    each_head(0, heads, output)

    @pl.when(jnp.logical_not(first))
    def _():
        each_head(0, heads, lambda h: send_query(h).wait_send())

    @pl.when(jnp.logical_not(last))
    def _():
        each_head(0, heads, lambda h: send_result(h).wait_send())
        send_stats().wait_send()

    each_peer(lambda peer: whole_grad(peer).wait_send())
    each_peer(lambda peer: send_weights(peer, me).wait_send())
    each_head(0, heads, lambda h: pltpu.make_async_copy(
        outb.at[h], out_hbm.at[:, cols(h)], out_sem.at[h]).wait())


def shards(queries, keys, values, rates, fast_weights, momentum):
    n = lax.axis_size("seq")
    tok = queries.shape[0]
    heads = rates.shape[0]
    d = fast_weights.shape[0]
    own = momentum.shape[0]
    stat_rows = -(-heads // 8) * 8

    def by_head(x):
        return jnp.transpose(x, (1, 0, 2, 3)).reshape(heads, x.shape[0], 3 * d)

    mine = lax.dynamic_slice_in_dim(fast_weights, lax.axis_index("seq") * own, own, 0)
    vmem = pl.BlockSpec(memory_space=pltpu.VMEM)
    hbm = pl.BlockSpec(memory_space=pl.ANY)
    dma = pltpu.SemaphoreType.DMA
    out, weights, moments = pl.pallas_call(
        functools.partial(kernel, n, heads, tok, d, own),
        out_shape=(
            jax.ShapeDtypeStruct(queries.shape, BF16),
            jax.ShapeDtypeStruct((heads, own, 3 * d), BF16),
            jax.ShapeDtypeStruct((heads, own, 3 * d), F32),
        ),
        in_specs=[hbm, hbm, hbm, vmem, vmem, vmem, vmem],
        out_specs=(hbm, vmem, vmem),
        scratch_shapes=[
            pltpu.VMEM((heads, tok, d), BF16),
            pltpu.VMEM((heads, tok, d), BF16),
            pltpu.VMEM((heads, tok, d), BF16),
            pltpu.VMEM((heads, WIN, d), BF16),
            pltpu.VMEM((heads, tok, d), F32),
            pltpu.VMEM((heads, WIN, d), F32),
            pltpu.VMEM((heads, WIN, d), BF16),
            pltpu.VMEM((heads, WIN, d), BF16),
            pltpu.VMEM((WIN, 128), F32),
            pltpu.VMEM((stat_rows, WIN), F32),
            pltpu.VMEM((stat_rows, WIN), F32),
            pltpu.VMEM((heads, tok, d), BF16),
            pltpu.VMEM((tok, 4 * d), BF16),
            pltpu.VMEM((n, heads, own, 3 * d), BF16),
            pltpu.VMEM((n, heads, own, 3 * d), BF16),
            pltpu.VMEM((n, heads, own, 3 * d), BF16),
            dma((3, heads)), dma((heads,)), dma((heads,)), dma((heads,)),
            dma((heads,)), dma((heads,)), dma, dma,
            dma((n,)), dma((n,)), dma((n,)), dma((n,)),
        ],
        compiler_params=pltpu.CompilerParams(
            collective_id=0, has_side_effects=True, vmem_limit_bytes=60 * 1024 * 1024),
    )(queries, keys, values, jnp.transpose(rates), by_head(fast_weights), by_head(mine),
      by_head(momentum))

    def by_row(x):
        return jnp.transpose(x.reshape(heads, own, 3, d), (1, 0, 2, 3))

    return (out, by_row(weights), by_row(moments))


def solution(mesh):
    return jax.shard_map(
        shards,
        mesh=mesh,
        in_specs=(
            P(("groups", "seq"), ("head", "rep")),
            P(("groups", "seq"), ("head", "rep")),
            P(("groups", "seq"), ("head", "rep")),
            P(("head", "rep"), ("groups", "seq")),
            P(None, ("head", "rep"), None, None),
            P("seq", ("head", "rep"), None, None),
        ),
        out_specs=(
            P(("groups", "seq"), ("head", "rep")),
            P(("groups", "seq"), ("head", "rep"), None, None),
            P(("groups", "seq"), ("head", "rep"), None, None),
        ),
        check_vma=False,
    )
```

time: 393 us -> 106 us (0.27)
  the two profiles are of different devices: /device:TPU:0 before, /device:TPU:16 now
where the time goes in v1:
time: 106 us
  Pallas kernels  91.4 us (86%)
  local copies, waits for them, and re-layouts  13.8 us (13%)
    pallas_call x1, Pallas kernels, shards(): pl.pallas_call(functools.partial(kernel, n, heads, tok, d, own), out_shap...  91.4 us
    unnamed x11, local copies, waits for them, and re-layouts  6.68 us
    reshape x3, local copies, waits for them, and re-layouts, by_head(): return jnp.transpose(x, (1, 0, 2, 3)).reshape(heads, x.shape[0], 3 * d)  3.89 us
    reshape x2, local copies, waits for them, and re-layouts, by_row(): return jnp.transpose(x.reshape(heads, own, 3, d), (1, 0, 2, 3))  3.22 us

profile of v1, /device:TPU:16, one launch (start us, length us, event | category | flops | bytes accessed | tf_op | source)
XLA Modules:
  0.0 105.9 jit_solution(12156457771600933314)
XLA Ops:
  0.6 0.0 copy-start
  0.6 0.0 copy-start.2
  0.7 1.8 %copy_bitcast_fusion.1.wown_ref = bf16[10,32,384]{2,1,0:T(8,128)(2,1)} fusion(bf16[128,10,3,128]{3,0,2,1:T(8,128)(2,1)} %param.10, s32[]{:T(128)S(6)} %select_n.3), kind=kLoop, calls=%fused_computation.1 | loop fusion | bytes 491524 | tf_op jit(solution)/shard_map/reshape | solution.py:316
  2.4 0.0 copy-done
  2.4 0.8 copy_bitcast_fusion.mom_ref
  3.3 1.9 %copy.15 = f32[10,1024]{0,1:T(8,128)} copy(f32[10,1024]{1,0:T(8,128)} %param.9) | data formatting | bytes 81920 | tf_op args[3]
  5.1 0.0 copy-done.2
  5.1 0.6 copy.16
  5.8 1.3 %copy.19.w_ref = bf16[10,128,384]{2,1,0:T(8,128)(2,1)} copy(bf16[10,128,384]{1,2,0:T(8,128)(2,1)S(1)} %bitcast.18) | data formatting | bytes 1966080 | tf_op jit(solution)/shard_map/reshape | solution.py:316
  7.1 91.4 %shard_map.85 = (bf16[1024,1280]{1,0:T(8,128)(2,1)}, bf16[10,32,384]{2,1,0:T(8,128)(2,1)}, f32[10,32,384]{2,1,0:T(8,128)}) custom-call(bf16[1024,1280]{1,0:T(8,128)(2,1)} %q_hbm.1, bf16[1024,1280]{1,0:T(8,128)(2,1)} %k_hbm.1, bf16[1024,1280]{1,0:T(8,128)(2,1)} %v_hbm.1, f32[1024,10]{1,0:T(8,128)} %bitcast.20, bf16[10,128,384]{2,1,0:T(8,128)(2,1)} %copy.19.w_ref, ...), custom_call_target="tpu_custom_call" | custom-call | tf_op jit(solution)/shard_map/pallas_call | solution.py:322
  98.5 0.0 copy-start.1
  98.5 1.2 %reshape.24 = bf16[10,32,3,128]{3,2,1,0:T(4,128)(2,1)S(1)} reshape(bf16[10,32,384]{2,1,0:T(8,128)(2,1)} %get-tuple-element.7) | data formatting | bytes 491520 | tf_op jit(solution)/shard_map/reshape | solution.py:358
  99.7 0.7 copy.20
  100.4 2.1 %reshape.25 = f32[10,32,3,128]{3,2,1,0:T(4,128)} reshape(f32[10,32,384]{2,1,0:T(8,128)} %get-tuple-element.8) | data formatting | bytes 983040 | tf_op jit(solution)/shard_map/reshape | solution.py:358
  102.5 1.9 %copy.21 = f32[32,10,3,128]{3,0,2,1:T(8,128)} copy(f32[32,10,3,128]{3,2,0,1:T(4,128)} %bitcast.19) | data formatting | bytes 983040
  104.4 0.0 copy-done.1
  104.4 1.5 %copy.27 = bf16[1024,1280]{1,0:T(8,128)(2,1)} copy(bf16[1024,1280]{1,0:T(8,128)(2,1)S(1)} %copy-done.1) | data formatting | bytes 5242880
Async XLA Ops:
  0.6 1.8 %copy-start = (f32[32,10,3,128]{3,0,2,1:T(8,128)S(1)}, f32[32,10,3,128]{3,0,2,1:T(8,128)}, u32[]{:S(2)}) copy-start(f32[32,10,3,128]{3,0,2,1:T(8,128)} %param.11) | copy-start | bytes 1474564
  0.6 4.5 %copy-start.2 = (bf16[128,10,3,128]{3,0,2,1:T(8,128)(2,1)S(1)}, bf16[128,10,3,128]{3,0,2,1:T(8,128)(2,1)}, u32[]{:S(2)}) copy-start(bf16[128,10,3,128]{3,0,2,1:T(8,128)(2,1)} %param.10) | copy-start | bytes 2949124
  98.5 5.9 %copy-start.1 = (bf16[1024,1280]{1,0:T(8,128)(2,1)S(1)}, bf16[1024,1280]{1,0:T(8,128)(2,1)}, u32[]{:S(2)}) copy-start(bf16[1024,1280]{1,0:T(8,128)(2,1)} %get-tuple-element.15) | copy-start | bytes 7864324

commit v2 on v1

--- a/solution.py
+++ b/solution.py
@@ -32,11 +32,11 @@
 
 def kernel(
     n, heads, tok, d, own,
-    q_hbm, k_hbm, v_hbm, r_ref, w_ref, wown_ref, mom_ref,
+    q_hbm, k_hbm, v_hbm, r_ref, w_hbm, mom_ref,
     out_hbm, nw_ref, nm_ref,
-    qb, kb, vb, qr, att, lse, osend, orecv, stat, ssend, srecv, outb,
+    rateb, wb, wown, qb, kb, vb, qr, att, lse, osend, orecv, stat, ssend, srecv, outb,
     gradb, gbuf, rsbuf, wnew,
-    load_sem, out_sem, qs_sem, qr_sem, os_sem, or_sem, ss_sem, sr_sem,
+    w_sem, load_sem, out_sem, qs_sem, qr_sem, os_sem, or_sem, ss_sem, sr_sem,
     rs_s, rs_r, ag_s, ag_r,
 ):
     me = lax.axis_index("seq")
@@ -71,27 +71,42 @@
             src_ref=ssend, dst_ref=srecv, send_sem=ss_sem, recv_sem=sr_sem,
             device_id={"seq": after}, device_id_type=MESH)
 
-    def send_grad(peer, h):
+    def send_grad(j, step, h=None):
+        peer = jnp.clip(me + step, 0, n - 1)
+        slot = j if step == 1 else jnp.where(peer == j, n, j)
+        src, dst = gbuf.at[j], rsbuf.at[slot]
+        if h is not None:
+            src, dst = gbuf.at[j, h], rsbuf.at[slot, h]
         return pltpu.make_async_remote_copy(
-            src_ref=gbuf.at[peer, h], dst_ref=rsbuf.at[me, h],
-            send_sem=rs_s.at[peer], recv_sem=rs_r.at[me],
+            src_ref=src, dst_ref=dst, send_sem=rs_s.at[j], recv_sem=rs_r.at[slot],
             device_id={"seq": peer}, device_id_type=MESH)
 
-    def whole_grad(peer):
+    def arrived(slot):
+        pltpu.make_async_remote_copy(
+            src_ref=gbuf.at[0], dst_ref=rsbuf.at[slot], send_sem=rs_s.at[0],
+            recv_sem=rs_r.at[slot], device_id={"seq": before}, device_id_type=MESH).wait_recv()
+
+    def send_weights(j, step):
+        peer = before if step < 0 else after
         return pltpu.make_async_remote_copy(
-            src_ref=gbuf.at[peer], dst_ref=rsbuf.at[peer],
-            send_sem=rs_s.at[peer], recv_sem=rs_r.at[peer],
+            src_ref=wnew.at[j], dst_ref=wnew.at[j],
+            send_sem=ag_s.at[0 if step < 0 else 1, j], recv_sem=ag_r.at[j],
             device_id={"seq": peer}, device_id_type=MESH)
 
-    def send_weights(peer, slot):
-        return pltpu.make_async_remote_copy(
-            src_ref=wnew.at[me], dst_ref=wnew.at[slot],
-            send_sem=ag_s.at[peer], recv_sem=ag_r.at[slot],
-            device_id={"seq": peer}, device_id_type=MESH)
-
-    def each_peer(act):
-        for step in range(1, n):
-            act(lax.rem(me + step, n))
+    def relay(step):
+        for j in range(n) if step < 0 else reversed(range(n)):
+            @pl.when(j < me if step < 0 else j > me)
+            def _():
+                arrived(j)
+                def add(h, carry):
+                    gbuf[j, h] = (gbuf[j, h].astype(F32) + rsbuf[j, h].astype(F32)).astype(BF16)
+                    return carry
+                lax.fori_loop(0, heads, add, 0)
+                send_grad(j, step).start()
+
+    inner = jnp.logical_and(me > 0, me < n - 1)
+    near = jnp.logical_and(inner, me < n // 2)
+    far = jnp.logical_and(inner, me >= n // 2)
 
     def each_head(lo, hi, act):
         def body(h, carry):
@@ -103,11 +118,30 @@
         load(1, h).start()
         load(2, h).start()
 
+    own_rows = pl.ds(pl.multiple_of(me * own, own), own)
+    load_weights = pltpu.make_async_copy(w_hbm, wb, w_sem.at[0])
+    load_own = pltpu.make_async_copy(w_hbm.at[:, :, own_rows, :], wown, w_sem.at[1])
+    load_weights.start()
     each_head(0, heads, start_loads)
+    load_own.start()
     barrier = pltpu.get_barrier_semaphore()
-    each_peer(lambda peer: pl.semaphore_signal(
-        barrier, inc=1, device_id={"seq": peer}, device_id_type=MESH))
-    pl.semaphore_wait(barrier, n - 1)
+
+    @pl.when(jnp.logical_not(first))
+    def _():
+        pl.semaphore_signal(barrier, inc=1, device_id={"seq": before}, device_id_type=MESH)
+
+    @pl.when(jnp.logical_not(last))
+    def _():
+        pl.semaphore_signal(barrier, inc=1, device_id={"seq": after}, device_id_type=MESH)
+
+    @pl.when(inner)
+    def _():
+        pl.semaphore_wait(barrier, 2)
+
+    @pl.when(jnp.logical_not(inner))
+    def _():
+        pl.semaphore_wait(barrier, 1)
+
     early = heads // 2
 
     @pl.when(jnp.logical_not(first))
@@ -123,16 +157,15 @@
     def gradient(h):
         load(1, h).wait()
         load(2, h).wait()
-        weights = w_ref[h]
-        lane = lax.broadcasted_iota(jnp.int32, (ROWS, heads), 1)
-        total = jnp.zeros((d, 3 * d), F32)
+        weights = jnp.concatenate([wb[h, c] for c in range(3)], axis=1)
+        lane = lax.broadcasted_iota(jnp.int32, (ROWS, 128), 1)
         for b in range(tok // ROWS):
             part = slice(b * ROWS, (b + 1) * ROWS)
             keys = kb[h, part]
-            rate = jnp.sum(jnp.where(lane == h, r_ref[part], 0.0), axis=1, keepdims=True)
+            rate = jnp.sum(jnp.where(lane == h, rateb[part], 0.0), axis=1, keepdims=True)
             scaled = (vb[h, part].astype(F32) * rate).astype(BF16)
-            inner = dot_nn(keys, weights[:, : 2 * d])
-            gating, upward = inner[:, :d], inner[:, d:]
+            pair = dot_nn(keys, weights[:, : 2 * d])
+            gating, upward = pair[:, :d], pair[:, d:]
             sig = jax.nn.sigmoid(gating)
             silu = gating * sig
             hidden_grad = dot_nn(scaled, weights[:, 2 * d :])
@@ -144,10 +177,24 @@
         two = dot_tn(gradb[:, 3 * d :], gradb[:, 2 * d : 3 * d])
         for p in range(n):
             part = slice(p * own, (p + 1) * own)
-            gbuf[p, h, :, : 2 * d] = one[part].astype(BF16)
-            gbuf[p, h, :, 2 * d :] = two[part].astype(BF16)
-        each_peer(lambda peer: send_grad(peer, h).start())
-
+            gbuf[p, h, 0] = one[part, :d].astype(BF16)
+            gbuf[p, h, 1] = one[part, d:].astype(BF16)
+            gbuf[p, h, 2] = two[part].astype(BF16)
+
+        @pl.when(first)
+        def _():
+            for j in reversed(range(1, n)):
+                send_grad(j, 1, h).start()
+
+        @pl.when(last)
+        def _():
+            for j in range(n - 1):
+                send_grad(j, -1, h).start()
+
+    held_rates = jnp.concatenate(
+        [r_ref[...], jnp.zeros((128 - heads, tok), F32)], axis=0)
+    rateb[...] = jnp.transpose(held_rates)
+    load_weights.wait()
     each_head(0, heads, gradient)
 
     @pl.when(jnp.logical_not(first))
@@ -203,7 +250,26 @@
                 o = inside(h, b)
             att[h, part] = o
 
-    each_head(0, heads, local)
+    each_head(0, early, local)
+
+    @pl.when(near)
+    def _():
+        relay(1)
+
+    @pl.when(far)
+    def _():
+        relay(-1)
+
+    each_head(early, heads, local)
+
+    @pl.when(near)
+    def _():
+        relay(-1)
+
+    @pl.when(far)
+    def _():
+        relay(1)
+
     tail = tok - WIN
 
     def remote(h):
@@ -222,28 +288,41 @@
         stat[...] = jnp.zeros_like(stat)
         each_head(0, early, remote)
 
-    each_peer(lambda peer: whole_grad(peer).wait_recv())
+    @pl.when(jnp.logical_not(first))
+    def _():
+        arrived(me)
+
+    @pl.when(jnp.logical_not(last))
+    def _():
+        arrived(n)
+
+    load_own.wait()
 
     def refresh(h):
-        total = gbuf[me, h].astype(F32)
-        for step in range(1, n):
-            total = total + rsbuf[lax.rem(me + step, n), h].astype(F32)
-        moment = momentum_keep * mom_ref[h] + total
-        nm_ref[h] = moment
-        old = wown_ref[h].astype(F32)
-        moved = old + moment
         for c in range(3):
-            part = slice(c * d, (c + 1) * d)
-            o, m = old[:, part], moved[:, part]
+            total = gbuf[me, h, c].astype(F32)
+            total = total + jnp.where(first, 0.0, rsbuf[me, h, c].astype(F32))
+            total = total + jnp.where(last, 0.0, rsbuf[n, h, c].astype(F32))
+            moment = momentum_keep * mom_ref[h, c] + total
+            nm_ref[h, c] = moment
+            o = wown[h, c].astype(F32)
+            m = o + moment
             ratio = jnp.sqrt(
                 (jnp.mean(o * o, axis=1, keepdims=True) + epsilon)
                 / (jnp.mean(m * m, axis=1, keepdims=True) + epsilon))
             new = (m * ratio).astype(BF16)
-            wnew[me, h, :, part] = new
-            nw_ref[h, :, part] = new
+            wnew[me, h, c] = new
+            nw_ref[h, c] = new
 
     each_head(0, heads, refresh)
-    each_peer(lambda peer: send_weights(peer, me).start())
+
+    @pl.when(jnp.logical_not(last))
+    def _():
+        send_weights(me, 1).start()
+
+    @pl.when(jnp.logical_not(first))
+    def _():
+        send_weights(me, -1).start()
 
     @pl.when(jnp.logical_not(last))
     def _():
@@ -251,7 +330,23 @@
         ssend[...] = jnp.transpose(stat[...])[: ssend.shape[0]]
         send_stats().start()
 
-    each_peer(lambda peer: send_weights(peer, peer).wait_recv())
+    for step in range(1, n):
+        @pl.when(me >= step)
+        def _():
+            send_weights(me - step, 1).wait_recv()
+
+            @pl.when(jnp.logical_not(last))
+            def _():
+                send_weights(me - step, 1).start()
+
+        @pl.when(me + step < n)
+        def _():
+            send_weights(me + step, -1).wait_recv()
+
+            @pl.when(jnp.logical_not(first))
+            def _():
+                send_weights(me + step, -1).start()
+
 
     @pl.when(jnp.logical_not(first))
     def _():
@@ -277,11 +372,12 @@
                     att[h, part] * mine + orecv[h, part].astype(F32) * other) / (mine + other)
 
         weights = jnp.concatenate(
-            [wnew[p, h].astype(F32) for p in range(n)], axis=0).astype(BF16)
+            [jnp.concatenate([wnew[p, h, c].astype(F32) for p in range(n)], axis=0)
+             for c in range(3)], axis=1).astype(BF16)
         for b in range(tok // ROWS):
             part = slice(b * ROWS, (b + 1) * ROWS)
-            inner = dot_nn(qb[h, part], weights[:, : 2 * d])
-            gating, upward = inner[:, :d], inner[:, d:]
+            pair = dot_nn(qb[h, part], weights[:, : 2 * d])
+            gating, upward = pair[:, :d], pair[:, d:]
             hidden = (gating * jax.nn.sigmoid(gating) * upward).astype(BF16)
             fast = dot_nt(hidden, weights[:, 2 * d :])
             outb[h, part] = (fast + att[h, part]).astype(BF16)
@@ -298,8 +394,19 @@
         each_head(0, heads, lambda h: send_result(h).wait_send())
         send_stats().wait_send()
 
-    each_peer(lambda peer: whole_grad(peer).wait_send())
-    each_peer(lambda peer: send_weights(peer, me).wait_send())
+    for j in range(n):
+        @pl.when(j != me)
+        def _():
+            send_grad(j, 1).wait_send()
+
+        @pl.when(jnp.logical_and(j <= me, me < n - 1))
+        def _():
+            send_weights(j, 1).wait_send()
+
+        @pl.when(jnp.logical_and(j >= me, me > 0))
+        def _():
+            send_weights(j, -1).wait_send()
+
     each_head(0, heads, lambda h: pltpu.make_async_copy(
         outb.at[h], out_hbm.at[:, cols(h)], out_sem.at[h]).wait())
 
@@ -313,9 +420,11 @@
     stat_rows = -(-heads // 8) * 8
 
     def by_head(x):
-        return jnp.transpose(x, (1, 0, 2, 3)).reshape(heads, x.shape[0], 3 * d)
-
-    mine = lax.dynamic_slice_in_dim(fast_weights, lax.axis_index("seq") * own, own, 0)
+        return jnp.transpose(x, (1, 2, 0, 3))
+
+    def by_row(x):
+        return jnp.transpose(x, (2, 0, 1, 3))
+
     vmem = pl.BlockSpec(memory_space=pltpu.VMEM)
     hbm = pl.BlockSpec(memory_space=pl.ANY)
     dma = pltpu.SemaphoreType.DMA
@@ -323,12 +432,15 @@
         functools.partial(kernel, n, heads, tok, d, own),
         out_shape=(
             jax.ShapeDtypeStruct(queries.shape, BF16),
-            jax.ShapeDtypeStruct((heads, own, 3 * d), BF16),
-            jax.ShapeDtypeStruct((heads, own, 3 * d), F32),
+            jax.ShapeDtypeStruct((heads, 3, own, d), BF16),
+            jax.ShapeDtypeStruct((heads, 3, own, d), F32),
         ),
-        in_specs=[hbm, hbm, hbm, vmem, vmem, vmem, vmem],
+        in_specs=[hbm, hbm, hbm, vmem, hbm, vmem],
         out_specs=(hbm, vmem, vmem),
         scratch_shapes=[
+            pltpu.VMEM((tok, 128), F32),
+            pltpu.VMEM((heads, 3, d, d), BF16),
+            pltpu.VMEM((heads, 3, own, d), BF16),
             pltpu.VMEM((heads, tok, d), BF16),
             pltpu.VMEM((heads, tok, d), BF16),
             pltpu.VMEM((heads, tok, d), BF16),
@@ -342,20 +454,16 @@
             pltpu.VMEM((stat_rows, WIN), F32),
             pltpu.VMEM((heads, tok, d), BF16),
             pltpu.VMEM((tok, 4 * d), BF16),
-            pltpu.VMEM((n, heads, own, 3 * d), BF16),
-            pltpu.VMEM((n, heads, own, 3 * d), BF16),
-            pltpu.VMEM((n, heads, own, 3 * d), BF16),
-            dma((3, heads)), dma((heads,)), dma((heads,)), dma((heads,)),
+            pltpu.VMEM((n, heads, 3, own, d), BF16),
+            pltpu.VMEM((n + 1, heads, 3, own, d), BF16),
+            pltpu.VMEM((n, heads, 3, own, d), BF16),
+            dma((2,)), dma((3, heads)), dma((heads,)), dma((heads,)), dma((heads,)),
             dma((heads,)), dma((heads,)), dma, dma,
-            dma((n,)), dma((n,)), dma((n,)), dma((n,)),
+            dma((n,)), dma((n + 1,)), dma((2, n)), dma((n,)),
         ],
         compiler_params=pltpu.CompilerParams(
             collective_id=0, has_side_effects=True, vmem_limit_bytes=60 * 1024 * 1024),
-    )(queries, keys, values, jnp.transpose(rates), by_head(fast_weights), by_head(mine),
-      by_head(momentum))
-
-    def by_row(x):
-        return jnp.transpose(x.reshape(heads, own, 3, d), (1, 0, 2, 3))
+    )(queries, keys, values, rates, by_head(fast_weights), by_head(momentum))
 
     return (out, by_row(weights), by_row(moments))
 

time: 106 us -> 110 us (1.038)
  the two profiles are of different devices: /device:TPU:16 before, /device:TPU:26 now
where the time goes in v2:
time: 110 us
  Pallas kernels  104 us (95%)
  local copies, waits for them, and re-layouts  4.95 us (4%)
    pallas_call x1, Pallas kernels, shards(): pl.pallas_call(functools.partial(kernel, n, heads, tok, d, own), out_shap...  104 us
    unnamed x7, local copies, waits for them, and re-layouts  4.95 us

profile of v2, /device:TPU:26, one launch (start us, length us, event | category | flops | bytes accessed | tf_op | source)
XLA Modules:
  0.0 109.8 jit_solution(5240601634906764564)
XLA Ops:
  0.6 104.2 %shard_map.85 = (bf16[1024,1280]{1,0:T(8,128)(2,1)}, bf16[10,3,32,128]{3,2,1,0:T(8,128)(2,1)}, f32[10,3,32,128]{3,2,1,0:T(8,128)}) custom-call(bf16[1024,1280]{1,0:T(8,128)(2,1)} %q_hbm.1, bf16[1024,1280]{1,0:T(8,128)(2,1)} %k_hbm.1, bf16[1024,1280]{1,0:T(8,128)(2,1)} %v_hbm.1, f32[10,1024]{1,0:T(8,128)} %r_ref.1, bf16[10,3,128,128]{3,2,1,0:T(8,128)(2,1)} %bitcast.4, ...), custom_call_target="tpu_custom_call" | custom-call | tf_op jit(solution)/shard_map/pallas_call | solution.py:431
  104.9 0.0 copy-start.1
  104.9 0.0 copy-start
  104.9 3.5 %copy.12 = bf16[1024,1280]{1,0:T(8,128)(2,1)} copy(bf16[1024,1280]{1,0:T(8,128)(2,1)} %get-tuple-element.12) | data formatting | bytes 5242880
  108.4 0.0 copy-done.1
  108.4 0.7 copy.13
  109.1 0.0 copy-done
  109.1 0.8 copy.14
Async XLA Ops:
  104.9 3.5 %copy-start.1 = (bf16[10,3,32,128]{3,2,1,0:T(8,128)(2,1)S(1)}, bf16[10,3,32,128]{3,2,1,0:T(8,128)(2,1)}, u32[]{:S(2)}) copy-start(bf16[10,3,32,128]{3,2,1,0:T(8,128)(2,1)} %get-tuple-element.7) | copy-start | bytes 737284
  104.9 4.2 %copy-start = (f32[10,3,32,128]{3,2,1,0:T(8,128)S(1)}, f32[10,3,32,128]{3,2,1,0:T(8,128)}, u32[]{:S(2)}) copy-start(f32[10,3,32,128]{3,2,1,0:T(8,128)} %get-tuple-element.8) | copy-start | bytes 1474564

commit v3 on v2

--- a/solution.py
+++ b/solution.py
@@ -142,9 +142,15 @@
     def _():
         pl.semaphore_wait(barrier, 1)
 
-    early = heads // 2
-
-    @pl.when(jnp.logical_not(first))
+    early = heads * 7 // 10
+    ahead = heads * 4 // 10
+    left_half = me < n // 2
+    r0 = jnp.where(last, 0, jnp.where(left_half, ahead, 0))
+    r1 = jnp.where(last, 0, jnp.where(left_half, early, ahead))
+    r2 = jnp.where(last, 0, early)
+    r3 = jnp.where(last, 0, heads)
+
+    @pl.when(inner)
     def _():
         each_head(0, early, lambda h: send_query(h).start())
 
@@ -197,9 +203,9 @@
     load_weights.wait()
     each_head(0, heads, gradient)
 
-    @pl.when(jnp.logical_not(first))
-    def _():
-        each_head(early, heads, lambda h: send_query(h).start())
+    @pl.when(jnp.logical_and(last, jnp.logical_not(first)))
+    def _():
+        each_head(0, early, lambda h: send_query(h).start())
 
     def with_ones(values, blocks):
         return jnp.concatenate([values, jnp.concatenate([ones] * blocks, axis=0)], axis=1)
@@ -250,26 +256,6 @@
                 o = inside(h, b)
             att[h, part] = o
 
-    each_head(0, early, local)
-
-    @pl.when(near)
-    def _():
-        relay(1)
-
-    @pl.when(far)
-    def _():
-        relay(-1)
-
-    each_head(early, heads, local)
-
-    @pl.when(near)
-    def _():
-        relay(-1)
-
-    @pl.when(far)
-    def _():
-        relay(1)
-
     tail = tok - WIN
 
     def remote(h):
@@ -283,10 +269,30 @@
             stat[part] = jnp.where(lane == h, s, stat[part])
         send_result(h).start()
 
-    @pl.when(jnp.logical_not(last))
-    def _():
-        stat[...] = jnp.zeros_like(stat)
-        each_head(0, early, remote)
+    stat[...] = jnp.zeros_like(stat)
+    each_head(0, r0, remote)
+    each_head(0, heads // 2, local)
+
+    @pl.when(near)
+    def _():
+        relay(1)
+
+    @pl.when(far)
+    def _():
+        relay(-1)
+
+    each_head(heads // 2, heads, local)
+    each_head(r0, r1, remote)
+
+    @pl.when(near)
+    def _():
+        relay(-1)
+
+    @pl.when(far)
+    def _():
+        relay(1)
+
+    each_head(r1, r2, remote)
 
     @pl.when(jnp.logical_not(first))
     def _():
@@ -324,13 +330,11 @@
     def _():
         send_weights(me, -1).start()
 
-    @pl.when(jnp.logical_not(last))
-    def _():
-        each_head(early, heads, remote)
-        ssend[...] = jnp.transpose(stat[...])[: ssend.shape[0]]
-        send_stats().start()
-
-    for step in range(1, n):
+    @pl.when(jnp.logical_not(first))
+    def _():
+        each_head(early, heads, lambda h: send_query(h).start())
+
+    def pass_weights(step):
         @pl.when(me >= step)
         def _():
             send_weights(me - step, 1).wait_recv()
@@ -347,6 +351,17 @@
             def _():
                 send_weights(me + step, -1).start()
 
+    if n > 1:
+        pass_weights(1)
+    each_head(r2, r3, remote)
+
+    @pl.when(jnp.logical_not(last))
+    def _():
+        ssend[...] = jnp.transpose(stat[...])[: ssend.shape[0]]
+        send_stats().start()
+
+    for step in range(2, n):
+        pass_weights(step)
 
     @pl.when(jnp.logical_not(first))
     def _():

time: 110 us -> 98.3 us (0.89)
  Pallas kernels: 104 us -> 92.5 us
    pallas_call x1, Pallas kernels: 104 us -> 92.5 us  [shards(): pl.pallas_call(functools.partial(kernel, n, heads, tok, d, own), out_shap...]
where the time goes in v3:
time: 98.3 us; the launch traced here: 98.1 us
  Pallas kernels  92.5 us (94%)
  local copies, waits for them, and re-layouts  4.95 us (5%)
    pallas_call x1, Pallas kernels, shards(): pl.pallas_call(functools.partial(kernel, n, heads, tok, d, own), out_shap...  92.5 us
    unnamed x7, local copies, waits for them, and re-layouts  4.95 us

profile of v3, /device:TPU:26, one launch (start us, length us, event | category | flops | bytes accessed | tf_op | source)
XLA Modules:
  0.0 98.1 jit_solution(6632667576623832315)
XLA Ops:
  0.6 92.5 %shard_map.85 = (bf16[1024,1280]{1,0:T(8,128)(2,1)}, bf16[10,3,32,128]{3,2,1,0:T(8,128)(2,1)}, f32[10,3,32,128]{3,2,1,0:T(8,128)}) custom-call(bf16[1024,1280]{1,0:T(8,128)(2,1)} %q_hbm.1, bf16[1024,1280]{1,0:T(8,128)(2,1)} %k_hbm.1, bf16[1024,1280]{1,0:T(8,128)(2,1)} %v_hbm.1, f32[10,1024]{1,0:T(8,128)} %r_ref.1, bf16[10,3,128,128]{3,2,1,0:T(8,128)(2,1)} %bitcast.4, ...), custom_call_target="tpu_custom_call" | custom-call | tf_op jit(solution)/shard_map/pallas_call | solution.py:446
  93.1 0.0 copy-start.1
  93.2 0.0 copy-start
  93.2 3.5 %copy.12 = bf16[1024,1280]{1,0:T(8,128)(2,1)} copy(bf16[1024,1280]{1,0:T(8,128)(2,1)} %get-tuple-element.12) | data formatting | bytes 5242880
  96.6 0.0 copy-done.1
  96.6 0.7 copy.13
  97.3 0.0 copy-done
  97.3 0.8 copy.14
Async XLA Ops:
  93.1 3.5 %copy-start.1 = (bf16[10,3,32,128]{3,2,1,0:T(8,128)(2,1)S(1)}, bf16[10,3,32,128]{3,2,1,0:T(8,128)(2,1)}, u32[]{:S(2)}) copy-start(bf16[10,3,32,128]{3,2,1,0:T(8,128)(2,1)} %get-tuple-element.7) | copy-start | bytes 737284
  93.2 4.2 %copy-start = (f32[10,3,32,128]{3,2,1,0:T(8,128)S(1)}, f32[10,3,32,128]{3,2,1,0:T(8,128)}, u32[]{:S(2)}) copy-start(f32[10,3,32,128]{3,2,1,0:T(8,128)} %get-tuple-element.8) | copy-start | bytes 1474564

commit v4 on v3

--- a/solution.py
+++ b/solution.py
@@ -142,8 +142,8 @@
     def _():
         pl.semaphore_wait(barrier, 1)
 
-    early = heads * 7 // 10
-    ahead = heads * 4 // 10
+    early = heads * 5 // 10
+    ahead = heads * 3 // 10
     left_half = me < n // 2
     r0 = jnp.where(last, 0, jnp.where(left_half, ahead, 0))
     r1 = jnp.where(last, 0, jnp.where(left_half, early, ahead))

time: 98.3 us -> 98.3 us (level)
  no operation moved by 1% of the time
where the time goes in v4:
time: 98.3 us; the launch traced here: 98.1 us
  Pallas kernels  92.5 us (94%)
  local copies, waits for them, and re-layouts  4.95 us (5%)
    pallas_call x1, Pallas kernels, shards(): pl.pallas_call(functools.partial(kernel, n, heads, tok, d, own), out_shap...  92.5 us
    unnamed x7, local copies, waits for them, and re-layouts  4.95 us

profile of v4, /device:TPU:26, one launch (start us, length us, event | category | flops | bytes accessed | tf_op | source)
XLA Modules:
  0.0 98.1 jit_solution(8833119672543894384)
XLA Ops:
  0.6 92.5 %shard_map.85 = (bf16[1024,1280]{1,0:T(8,128)(2,1)}, bf16[10,3,32,128]{3,2,1,0:T(8,128)(2,1)}, f32[10,3,32,128]{3,2,1,0:T(8,128)}) custom-call(bf16[1024,1280]{1,0:T(8,128)(2,1)} %q_hbm.1, bf16[1024,1280]{1,0:T(8,128)(2,1)} %k_hbm.1, bf16[1024,1280]{1,0:T(8,128)(2,1)} %v_hbm.1, f32[10,1024]{1,0:T(8,128)} %r_ref.1, bf16[10,3,128,128]{3,2,1,0:T(8,128)(2,1)} %bitcast.4, ...), custom_call_target="tpu_custom_call" | custom-call | tf_op jit(solution)/shard_map/pallas_call | solution.py:446
  93.1 0.0 copy-start.1
  93.2 0.0 copy-start
  93.2 3.5 %copy.12 = bf16[1024,1280]{1,0:T(8,128)(2,1)} copy(bf16[1024,1280]{1,0:T(8,128)(2,1)} %get-tuple-element.12) | data formatting | bytes 5242880
  96.6 0.0 copy-done.1
  96.6 0.7 copy.13
  97.3 0.0 copy-done
  97.3 0.8 copy.14
Async XLA Ops:
  93.1 3.5 %copy-start.1 = (bf16[10,3,32,128]{3,2,1,0:T(8,128)(2,1)S(1)}, bf16[10,3,32,128]{3,2,1,0:T(8,128)(2,1)}, u32[]{:S(2)}) copy-start(bf16[10,3,32,128]{3,2,1,0:T(8,128)(2,1)} %get-tuple-element.7) | copy-start | bytes 737284
  93.2 4.2 %copy-start = (f32[10,3,32,128]{3,2,1,0:T(8,128)S(1)}, f32[10,3,32,128]{3,2,1,0:T(8,128)}, u32[]{:S(2)}) copy-start(f32[10,3,32,128]{3,2,1,0:T(8,128)} %get-tuple-element.8) | copy-start | bytes 1474564
